TPU v7x, 512 devices: a whole 4x8x8 slice. The times are simulated.
512 devices in a mesh: section: 2 (over core), tensor: 32 (over z, x), dp: 8 (over y).
Axes of the slice: x: 4, y: 8, z: 8, core: 2. Of those that a mesh axis runs over, the one named last changes fastest.
Arguments:
- grad_out: bfloat16 [2048, 6144], P('dp', 'tensor'), may hold values from -6 to 6
- queries: bfloat16 [2, 2048, 4096], P('section', 'dp', 'tensor'), may hold values from -40 to 40
- key_rows: bfloat16 [2, 2048, 4096], P('section', 'dp', 'tensor'), may hold values from -40 to 40
- value_rows: bfloat16 [2, 2048, 4096], P('section', 'dp', 'tensor'), may hold values from -6 to 6
- w_qkv: bfloat16 [2, 6144, 12288], P('section', 'dp', 'tensor'), may hold values from -0.078125 to 0.078125
- w_out: bfloat16 [2, 4096, 6144], P('section', 'tensor', 'dp'), may hold values from -0.09375 to 0.09375
- seg_lengths: int32 [8, 3], P('dp'), may hold values from 0 to 128, as said below
Outputs:
- input_grad: bfloat16 [2, 2048, 6144], P('section', 'dp', 'tensor')
- out_weight_grad: bfloat16 [2, 4096, 6144], P('section', 'tensor', 'dp')
Inputs may be any that keep to these rules, and one draw needn't show every extreme that they name: `seg_lengths`: each row sums to 256, holds one image of exactly 128 patches and either a second of 128 patches and an empty last slot, or two of 64 patches.
All inputs are finite; a program needn't handle non-finite values.
Results may differ from a plain program's by a relative error of at most 0.023.
Values may be sent and summed in bfloat16 or wider, within the bound.
A program may use at most 64 MiB of HBM per device.

v0:
```python
import jax
import jax.numpy as jnp
from jax import lax
from jax.sharding import PartitionSpec as P

PACK = 256
MB = 1
negative_big = -1e30


def passed_along(value, axis, steps):
    count = lax.axis_size(axis)
    first, last = (max(0, -steps), min(count, count - steps))
    return lax.ppermute(value, axis, [(source, source + steps) for source in range(first, last)])


def contract(left, right, left_dim, right_dim):
    return lax.dot_general(
        left, right, (((left_dim,), (right_dim,)), ((), ())), preferred_element_type=jnp.float32
    )


def attend_back(query_blk, key_blk, value_blk, grad_attn, same_seg, scaling):
    scores = contract(query_blk, key_blk, 1, 1) * scaling
    scores = jnp.where(same_seg, scores, negative_big)
    peak = jnp.max(scores, axis=-1, keepdims=True)
    shifted = jnp.exp(scores - peak)
    probs = shifted / jnp.sum(shifted, axis=-1, keepdims=True)
    probs_low = probs.astype(jnp.bfloat16)
    attended = jnp.dot(probs_low, value_blk, preferred_element_type=jnp.float32).astype(
        jnp.bfloat16
    )
    grad_value = contract(probs_low, grad_attn, 0, 0).astype(jnp.bfloat16)
    grad_probs = contract(grad_attn, value_blk, 1, 1)
    centred = jnp.sum(probs * grad_probs, axis=-1, keepdims=True)
    grad_scores = (probs * (grad_probs - centred) * scaling).astype(jnp.bfloat16)
    grad_query = jnp.dot(grad_scores, key_blk, preferred_element_type=jnp.float32).astype(
        jnp.bfloat16
    )
    grad_key = contract(grad_scores, query_blk, 0, 0).astype(jnp.bfloat16)
    return (attended, grad_query, grad_key, grad_value)


def per_device(grad_out, queries, key_rows, value_rows, w_qkv, w_out, seg_lengths):
    sections = lax.axis_size("section")
    section_index = lax.axis_index("section")
    head_index = lax.axis_index("tensor")
    width = grad_out.shape[1]
    qkv_full, out_full = (
        lax.all_gather(w_qkv, "dp", axis=1, tiled=True),
        lax.all_gather(w_out, "dp", axis=2, tiled=True),
    )
    proj_in = qkv_full[0]
    proj_out = out_full[0]
    head_dim = proj_out.shape[0]
    full_width = proj_out.shape[1]
    scaling = head_dim ** (-0.5)
    seg_ends = jnp.cumsum(seg_lengths, axis=1)
    position = jnp.arange(PACK, dtype=jnp.int32)
    seg_table = jnp.sum((position[None, :, None] >= seg_ends[:, None, :]).astype(jnp.int32), axis=2)
    offset = sections - 1 - section_index
    carried = jnp.zeros((PACK, width), jnp.bfloat16)
    result = jnp.zeros((MB * PACK, width), jnp.bfloat16)
    grad_acc = jnp.zeros((head_dim, full_width), jnp.float32)
    for step_index in range(MB + sections - 1):
        micro = step_index - offset
        active = (micro >= 0) & (micro < MB)
        which = jnp.clip(micro, 0, MB - 1)
        incoming = jnp.where(section_index == sections - 1, grad_out, carried)
        whole = lax.all_gather(incoming, "tensor", axis=1, tiled=True)
        query_blk = queries[0]
        key_blk = key_rows[0]
        value_blk = value_rows[0]
        seg_ids = lax.dynamic_index_in_dim(seg_table, which, 0, keepdims=False)
        same_seg = seg_ids[:, None] == seg_ids[None, :]
        grad_attn = contract(whole, proj_out, 1, 1).astype(jnp.bfloat16)
        attended, grad_query, grad_key, grad_value = attend_back(
            query_blk, key_blk, value_blk, grad_attn, same_seg, scaling
        )
        combined = jnp.concatenate([grad_query, grad_key, grad_value], axis=1)
        head_term = contract(combined, proj_in, 1, 1)
        summed = lax.psum(head_term.astype(jnp.bfloat16), "tensor").astype(jnp.float32)
        share = lax.dynamic_slice_in_dim(summed, head_index * width, width, 1)
        block_grad = (incoming.astype(jnp.float32) + share).astype(jnp.bfloat16)
        result = jnp.where(active, block_grad, result)
        grad_acc = grad_acc + jnp.where(active, contract(attended, whole, 0, 0), 0.0)
        carried = passed_along(block_grad, "section", -1)
    weight_share = lax.psum_scatter(
        grad_acc.astype(jnp.bfloat16), "dp", scatter_dimension=1, tiled=True
    )
    return (result[None], weight_share[None])


def solution(mesh):
    return jax.shard_map(
        per_device,
        mesh=mesh,
        in_specs=(
            P("dp", "tensor"),
            P("section", "dp", "tensor"),
            P("section", "dp", "tensor"),
            P("section", "dp", "tensor"),
            P("section", "dp", "tensor"),
            P("section", "tensor", "dp"),
            P("dp", None),
        ),
        out_specs=(P("section", "dp", "tensor"), P("section", "tensor", "dp")),
        check_vma=False,
    )
```

profile of v0, /device:TPU:6, one launch (start us, length us, event | category | flops | bytes accessed | tf_op | source)
XLA Modules:
  0.0 695.8 jit_solution(12003352529557310799)
XLA Ops:
  7.2 0.7 all-gather.7.cloned.1.call-update
  8.0 0.7 broadcast_select_fusion.1
  8.7 0.7 all-gather.9.cloned.1.call-update
  9.4 0.8 reduce_window_sum.11
  10.4 1.1 fusion.49
  11.5 45.2 %all-gather.7.cloned.1.call-done = bf16[1,128,6144]{2,1,0:T(8,128)(2,1)} async-done(((bf16[1,128,768]{2,1,0:T(8,128)(2,1)}), bf16[1,128,6144]{2,1,0:T(8,128)(2,1)}) %all-gather.7.cloned.1.call-update) | async-done | bytes 1572880 | tf_op jit(solution)/shard_map/all_gather | solution.py:51
  56.7 86.7 %all-gather.5.cloned.1.call-done = bf16[256,6144]{0,1:T(8,128)(2,1)} async-done(((bf16[256,192]{0,1:T(8,128)(2,1)}), bf16[256,6144]{0,1:T(8,128)(2,1)}) %all-gather.5.cloned.1.call-update) | async-done | bytes 3145744 | tf_op jit(solution)/shard_map/all_gather | solution.py:70
  143.4 3.4 fusion.9
  147.7 57.7 %all-gather.9.cloned.1.call-done = bf16[1,6144,384]{2,1,0:T(8,128)(2,1)} async-done(((bf16[1,768,384]{2,1,0:T(8,128)(2,1)}), bf16[1,6144,384]{2,1,0:T(8,128)(2,1)}) %all-gather.9.cloned.1.call-update) | async-done | bytes 4718608 | tf_op jit(solution)/shard_map/all_gather | solution.py:50
  205.5 5.9 convolution_convert_fusion.1
  211.5 168.1 %all-reduce.3.cloned.1.call-done = bf16[256,6144]{0,1:T(8,128)(2,1)} async-done(((bf16[256,6144]{0,1:T(8,128)(2,1)}), bf16[256,6144]{0,1:T(8,128)(2,1)}) %all-reduce.3.cloned.1.call-update) | async-done | bytes 3145744 | tf_op jit(solution)/shard_map/psum | solution.py:82
  379.6 0.9 add_convert_fusion.1
  380.5 1.3 collective-permute-start
  381.8 1.9 collective-permute-done
  384.4 82.7 %all-gather.11.cloned.1.call-done = bf16[256,6144]{0,1:T(8,128)(2,1)} async-done(((bf16[256,192]{0,1:T(8,128)(2,1)}), bf16[256,6144]{0,1:T(8,128)(2,1)}) %all-gather.11.cloned.1.call-update) | async-done | bytes 3145744 | tf_op jit(solution)/shard_map/all_gather | solution.py:70
  467.2 2.9 fusion.12
  471.0 5.9 convolution_convert_fusion
  477.3 1.6 copy-done.1
  478.8 1.2 convolution_select_fusion.1
  480.0 0.7 copy-done.2
  480.7 2.3 fusion.1
  483.1 160.8 %all-reduce.5.cloned.1.call-done = bf16[256,6144]{0,1:T(8,128)(2,1)} async-done(((bf16[256,6144]{0,1:T(8,128)(2,1)}), bf16[256,6144]{0,1:T(8,128)(2,1)}) %all-reduce.5.cloned.1.call-update) | async-done | bytes 3145744 | tf_op jit(solution)/shard_map/psum | solution.py:82
  644.0 1.6 fusion.28
  645.5 43.4 %reduce-scatter.2.cloned.1.call-done = bf16[128,768]{1,0:T(8,128)(2,1)} async-done(((bf16[128,6144]{1,0:T(8,128)(2,1)}), bf16[128,768]{1,0:T(8,128)(2,1)}) %reduce-scatter.2.cloned.1.call-update) | async-done | bytes 196624 | tf_op jit(solution)/shard_map/reduce_scatter | solution.py:88
  (44 shorter events, 3.2 us)
Async XLA Ops:
  7.2 139.7 %copy-start = (bf16[1,256,128]{2,1,0:T(8,128)(2,1)S(1)}, bf16[1,256,128]{2,1,0:T(8,128)(2,1)}, u32[]{:S(2)}) copy-start(bf16[1,256,128]{2,1,0:T(8,128)(2,1)} %param.10) | copy-start | bytes 196612
  7.2 49.5 %all-gather.7.cloned.1.call-start = ((), (), s32[]{:S(2)}) async-start(), calls=%async_computation.2 | async-start | bytes 1769472 | tf_op jit(solution)/shard_map/all_gather | solution.py:51
  7.9 135.5 %all-gather.5.cloned.1.call-start = ((), (), s32[]{:S(2)}) async-start(), calls=%async_computation.1 | async-start | bytes 3244032 | tf_op jit(solution)/shard_map/all_gather | solution.py:70
  8.7 196.8 %all-gather.9.cloned.1.call-start = ((), (), s32[]{:S(2)}) async-start(), calls=%async_computation.3 | async-start | bytes 5308416 | tf_op jit(solution)/shard_map/all_gather | solution.py:50
  9.4 370.2 %all-reduce.3.cloned.1.call-start = ((), (), s32[]{:S(2)}) async-start(), calls=%async_computation.4 | async-start | bytes 6291456 | tf_op jit(solution)/shard_map/psum | solution.py:82
  11.5 135.6 %copy-start.8 = (bf16[1,256,128]{2,1,0:T(8,128)(2,1)S(1)}, bf16[1,256,128]{2,1,0:T(8,128)(2,1)}, u32[]{:S(2)}) copy-start(bf16[1,256,128]{2,1,0:T(8,128)(2,1)} %param.8) | copy-start | bytes 196612
  11.5 135.8 %copy-start.9 = (bf16[1,256,128]{2,1,0:T(8,128)(2,1)S(1)}, bf16[1,256,128]{2,1,0:T(8,128)(2,1)}, u32[]{:S(2)}) copy-start(bf16[1,256,128]{2,1,0:T(8,128)(2,1)} %param.9) | copy-start | bytes 196612
  211.4 168.2 %copy-start.4 = (bf16[256,192]{0,1:T(8,128)(2,1)S(1)}, bf16[256,192]{0,1:T(8,128)(2,1)}, u32[]{:S(2)}) copy-start(bf16[256,192]{0,1:T(8,128)(2,1)} %param.7) | copy-start | bytes 294916
  211.4 255.8 %copy-start.3 = (bf16[1,128,6144]{2,1,0:T(8,128)(2,1)S(1)}, bf16[1,128,6144]{2,1,0:T(8,128)(2,1)}, u32[]{:S(2)}) copy-start(bf16[1,128,6144]{2,1,0:T(8,128)(2,1)} %all-gather.7.cloned.1.call-done) | copy-start | bytes 4718596
  211.4 255.8 %all-gather.11.cloned.1.call-start = ((), (), s32[]{:S(2)}) async-start(), calls=%async_computation.5 | async-start | bytes 3244032 | tf_op jit(solution)/shard_map/all_gather | solution.py:70
  380.5 90.0 %copy-start.6 = (bf16[256,192]{0,1:T(8,128)(2,1)}, bf16[256,192]{0,1:T(8,128)(2,1)S(1)}, u32[]{:S(2)}) copy-start(bf16[256,192]{0,1:T(8,128)(2,1)S(1)} %add_convert_fusion.1) | copy-start | bytes 294916
  380.5 3.2 collective-permute-start
  384.4 259.6 %all-reduce.5.cloned.1.call-start = ((), (), s32[]{:S(2)}) async-start(), calls=%async_computation.6 | async-start | bytes 6291456 | tf_op jit(solution)/shard_map/psum | solution.py:82
  477.0 1.9 copy-start.1
  477.0 212.0 %reduce-scatter.2.cloned.1.call-start = ((), (), s32[]{:S(2)}) async-start(), calls=%async_computation.7 | async-start | bytes 1769472 | tf_op jit(solution)/shard_map/reduce_scatter | solution.py:88
  478.8 1.9 copy-start.2
  480.7 163.2 %copy-start.5 = (bf16[256,192]{0,1:T(8,128)(2,1)S(1)}, bf16[256,192]{0,1:T(8,128)(2,1)}, u32[]{:S(2)}) copy-start(bf16[256,192]{0,1:T(8,128)(2,1)} %broadcast_select_fusion) | copy-start | bytes 294916
  480.7 163.2 %copy-start.7 = (bf16[256,192]{0,1:T(8,128)(2,1)S(1)}, bf16[256,192]{0,1:T(8,128)(2,1)}, u32[]{:S(2)}) copy-start(bf16[256,192]{0,1:T(8,128)(2,1)} %copy-done.6) | copy-start | bytes 294916
Sparse Core Ops, SparseCore 0:
  10.1 46.5 all-gather.6
  60.4 82.9 all-gather.4
  145.5 59.8 all-gather.8
  211.5 167.9 all-reduce.2
  384.5 82.6 all-gather.10
  477.1 166.8 all-reduce.4
  647.4 41.5 reduce-scatter.1
where the time goes:
time: 696 us
  waiting for transfers between devices  648 us (93%)
  matrix products  24.6 us (4%)
  between operations  14.3 us (2%)
    psum x2, waiting for transfers between devices, per_device(): lax.psum(head_term.astype(jnp.bfloat16), 'tensor').astype(jnp.float32)  329 us
    all_gather x2, waiting for transfers between devices, per_device(): whole = lax.all_gather(incoming, 'tensor', axis=1, tiled=True)  169 us
    all_gather x1, waiting for transfers between devices, per_device(): lax.all_gather(w_qkv, 'dp', axis=1, tiled=True)  57.7 us
    all_gather x1, waiting for transfers between devices, per_device(): lax.all_gather(w_out, 'dp', axis=2, tiled=True)  45.2 us
    reduce_scatter x1, waiting for transfers between devices, per_device(): lax.psum_scatter(grad_acc.astype(jnp.bfloat16), 'dp', scatter_dimension=1...  43.4 us
    dot_general x13, matrix products, contract(): lax.dot_general(left, right, (((left_dim,), (right_dim,)), ((), ())), pre...  23.9 us
  transfers between devices with their start and end apart: 8, of which 8 were waited for; matrix products, arithmetic and copies ran while one was open for 2% of the time, Pallas kernels for 0%

commit v1 on v0

--- a/solution.py
+++ b/solution.py
@@ -47,7 +47,9 @@
     head_index = lax.axis_index("tensor")
     width = grad_out.shape[1]
     qkv_full, out_full = (
-        lax.all_gather(w_qkv, "dp", axis=1, tiled=True),
+        jnp.concatenate(
+            lax.all_to_all(jnp.stack([w_qkv] * lax.axis_size("dp")), "dp", 0, 0), axis=1
+        ),
         lax.all_gather(w_out, "dp", axis=2, tiled=True),
     )
     proj_in = qkv_full[0]

time: 696 us -> 672 us (0.966)
  waiting for transfers between devices: 648 us -> 614 us
  starting transfers between devices: 1.57 us -> 8.78 us
    all_gather x1 -> x0, waiting for transfers between devices: 57.7 us -> none  [per_device(): lax.all_gather(w_qkv, 'dp', axis=1, tiled=True)]
    all_gather x1, waiting for transfers between devices: 45.2 us -> 71.1 us  [per_device(): lax.all_gather(w_out, 'dp', axis=2, tiled=True)]
    all_to_all x0 -> x1, starting transfers between devices: none -> 7.24 us  [per_device(): lax.all_to_all(jnp.stack([w_qkv] * lax.axis_size('dp')), 'dp', 0, 0)]
  transfers between devices with their start and end apart: 8 -> 8, of which waited for: 8 -> 7; matrix products, arithmetic and copies ran while one was open for 2% -> 2% of each run, Pallas kernels for 0% -> 0%
where the time goes in v1:
time: 672 us; the launch traced here: 671 us
  waiting for transfers between devices  614 us (91%)
  matrix products  23.4 us (3%)
  between operations  14.3 us (2%)
  starting transfers between devices  8.78 us (1%)
    psum x2, waiting for transfers between devices, per_device(): lax.psum(head_term.astype(jnp.bfloat16), 'tensor').astype(jnp.float32)  328 us
    all_gather x2, waiting for transfers between devices, per_device(): whole = lax.all_gather(incoming, 'tensor', axis=1, tiled=True)  170 us
    all_gather x1, waiting for transfers between devices, per_device(): lax.all_gather(w_out, 'dp', axis=2, tiled=True)  71.1 us
    reduce_scatter x1, waiting for transfers between devices, per_device(): lax.psum_scatter(grad_acc.astype(jnp.bfloat16), 'dp', scatter_dimension=1...  43.3 us
    dot_general x13, matrix products, contract(): lax.dot_general(left, right, (((left_dim,), (right_dim,)), ((), ())), pre...  22.7 us
  transfers between devices with their start and end apart: 8, of which 7 were waited for; matrix products, arithmetic and copies ran while one was open for 2% of the time, Pallas kernels for 0%

profile of v1, /device:TPU:6, one launch (start us, length us, event | category | flops | bytes accessed | tf_op | source)
XLA Modules:
  0.0 671.3 jit_solution(7230417291575023361)
XLA Ops:
  7.2 0.7 all-gather.6.cloned.1.call-update
  7.9 3.7 stack.2
  11.6 7.2 %all-to-all-start = ((bf16[8,1,768,384]{3,2,1,0:T(8,128)(2,1)}), bf16[8,1,768,384]{3,2,1,0:T(8,128)(2,1)}, u32[]{:S(2)}, u32[]{:S(2)}) async-start(bf16[8,1,768,384]{3,2,1,0:T(8,128)(2,1)} %stack.2), calls=%async_computation | async-start | bytes 9437184 | tf_op jit(solution)/shard_map/all_to_all | solution.py:51
  18.9 0.7 broadcast_select_fusion.1
  20.3 71.1 %all-gather.6.cloned.1.call-done = bf16[1,128,6144]{2,1,0:T(8,128)(2,1)} async-done(((bf16[1,128,768]{2,1,0:T(8,128)(2,1)}), bf16[1,128,6144]{2,1,0:T(8,128)(2,1)}) %all-gather.6.cloned.1.call-update) | async-done | bytes 1572880 | tf_op jit(solution)/shard_map/all_gather | solution.py:53
  91.3 87.0 %all-gather.4.cloned.1.call-done = bf16[256,6144]{0,1:T(8,128)(2,1)} async-done(((bf16[256,192]{0,1:T(8,128)(2,1)}), bf16[256,6144]{0,1:T(8,128)(2,1)}) %all-gather.4.cloned.1.call-update) | async-done | bytes 3145744 | tf_op jit(solution)/shard_map/all_gather | solution.py:72
  178.3 3.4 fusion.7
  182.6 5.8 convolution_convert_fusion.1
  188.5 166.9 %all-reduce.3.cloned.1.call-done = bf16[256,6144]{0,1:T(8,128)(2,1)} async-done(((bf16[256,6144]{0,1:T(8,128)(2,1)}), bf16[256,6144]{0,1:T(8,128)(2,1)}) %all-reduce.3.cloned.1.call-update) | async-done | bytes 3145744 | tf_op jit(solution)/shard_map/psum | solution.py:84
  355.4 0.9 add_convert_fusion.1
  356.3 1.3 collective-permute-start
  357.6 1.9 collective-permute-done
  359.5 0.7 broadcast_select_fusion
  360.2 82.7 %all-gather.8.cloned.1.call-done = bf16[256,6144]{0,1:T(8,128)(2,1)} async-done(((bf16[256,192]{0,1:T(8,128)(2,1)}), bf16[256,6144]{0,1:T(8,128)(2,1)}) %all-gather.8.cloned.1.call-update) | async-done | bytes 3145744 | tf_op jit(solution)/shard_map/all_gather | solution.py:72
  443.0 2.9 fusion.10
  446.8 5.8 convolution_convert_fusion
  452.7 0.2 convolution_convert_fusion.2
  452.9 1.6 copy-done.1
  454.5 1.2 convolution_select_fusion.1
  455.7 0.7 copy-done.2
  456.4 2.3 fusion.1
  458.7 160.9 %all-reduce.5.cloned.1.call-done = bf16[256,6144]{0,1:T(8,128)(2,1)} async-done(((bf16[256,6144]{0,1:T(8,128)(2,1)}), bf16[256,6144]{0,1:T(8,128)(2,1)}) %all-reduce.5.cloned.1.call-update) | async-done | bytes 3145744 | tf_op jit(solution)/shard_map/psum | solution.py:84
  619.6 1.6 fusion.26
  621.2 43.3 %reduce-scatter.2.cloned.1.call-done = bf16[128,768]{1,0:T(8,128)(2,1)} async-done(((bf16[128,6144]{1,0:T(8,128)(2,1)}), bf16[128,768]{1,0:T(8,128)(2,1)}) %reduce-scatter.2.cloned.1.call-update) | async-done | bytes 196624 | tf_op jit(solution)/shard_map/reduce_scatter | solution.py:90
  (46 shorter events, 2.7 us)
Async XLA Ops:
  7.2 174.5 %copy-start = (bf16[1,256,128]{2,1,0:T(8,128)(2,1)S(1)}, bf16[1,256,128]{2,1,0:T(8,128)(2,1)}, u32[]{:S(2)}) copy-start(bf16[1,256,128]{2,1,0:T(8,128)(2,1)} %param.10) | copy-start | bytes 196612
  7.2 84.1 %all-gather.6.cloned.1.call-start = ((), (), s32[]{:S(2)}) async-start(), calls=%async_computation.3 | async-start | bytes 1769472 | tf_op jit(solution)/shard_map/all_gather | solution.py:53
  11.6 7.3 %copy-start.4 = (bf16[256,192]{0,1:T(8,128)(2,1)S(1)}, bf16[256,192]{0,1:T(8,128)(2,1)}, u32[]{:S(2)}) copy-start(bf16[256,192]{0,1:T(8,128)(2,1)} %param.7) | copy-start | bytes 294916
  11.6 8.1 %copy-start.10 = (s32[1,3]{1,0:T(1,128)S(1)}, s32[1,3]{1,0:T(1,128)}, u32[]{:S(2)}) copy-start(s32[1,3]{1,0:T(1,128)} %param.13) | copy-start | bytes 40
  11.6 8.3 %copy-start.8 = (bf16[1,256,128]{2,1,0:T(8,128)(2,1)S(1)}, bf16[1,256,128]{2,1,0:T(8,128)(2,1)}, u32[]{:S(2)}) copy-start(bf16[1,256,128]{2,1,0:T(8,128)(2,1)} %param.8) | copy-start | bytes 196612
  11.6 8.3 %copy-start.9 = (bf16[1,256,128]{2,1,0:T(8,128)(2,1)S(1)}, bf16[1,256,128]{2,1,0:T(8,128)(2,1)}, u32[]{:S(2)}) copy-start(bf16[1,256,128]{2,1,0:T(8,128)(2,1)} %param.9) | copy-start | bytes 196612
  11.6 171.0 %all-to-all-start = ((bf16[8,1,768,384]{3,2,1,0:T(8,128)(2,1)}), bf16[8,1,768,384]{3,2,1,0:T(8,128)(2,1)}, u32[]{:S(2)}, u32[]{:S(2)}) async-start(bf16[8,1,768,384]{3,2,1,0:T(8,128)(2,1)} %stack.2), calls=%async_computation | async-start | bytes 9437184 | tf_op jit(solution)/shard_map/all_to_all | solution.py:51
  18.9 159.4 %all-gather.4.cloned.1.call-start = ((), (), s32[]{:S(2)}) async-start(), calls=%async_computation.2 | async-start | bytes 3244032 | tf_op jit(solution)/shard_map/all_gather | solution.py:72
  19.6 335.8 %all-reduce.3.cloned.1.call-start = ((), (), s32[]{:S(2)}) async-start(), calls=%async_computation.4 | async-start | bytes 6291456 | tf_op jit(solution)/shard_map/psum | solution.py:84
  188.4 254.6 %copy-start.3 = (bf16[1,128,6144]{2,1,0:T(8,128)(2,1)S(1)}, bf16[1,128,6144]{2,1,0:T(8,128)(2,1)}, u32[]{:S(2)}) copy-start(bf16[1,128,6144]{2,1,0:T(8,128)(2,1)} %all-gather.6.cloned.1.call-done) | copy-start | bytes 4718596
  188.4 254.6 %all-gather.8.cloned.1.call-start = ((), (), s32[]{:S(2)}) async-start(), calls=%async_computation.5 | async-start | bytes 3244032 | tf_op jit(solution)/shard_map/all_gather | solution.py:72
  356.3 90.0 %copy-start.6 = (bf16[256,192]{0,1:T(8,128)(2,1)}, bf16[256,192]{0,1:T(8,128)(2,1)S(1)}, u32[]{:S(2)}) copy-start(bf16[256,192]{0,1:T(8,128)(2,1)S(1)} %add_convert_fusion.1) | copy-start | bytes 294916
  356.3 3.2 collective-permute-start
  360.2 259.4 %all-reduce.5.cloned.1.call-start = ((), (), s32[]{:S(2)}) async-start(), calls=%async_computation.6 | async-start | bytes 6291456 | tf_op jit(solution)/shard_map/psum | solution.py:84
  452.6 1.9 copy-start.1
  452.6 211.8 %reduce-scatter.2.cloned.1.call-start = ((), (), s32[]{:S(2)}) async-start(), calls=%async_computation.7 | async-start | bytes 1769472 | tf_op jit(solution)/shard_map/reduce_scatter | solution.py:90
  454.5 1.9 copy-start.2
  456.4 163.2 %copy-start.5 = (bf16[256,192]{0,1:T(8,128)(2,1)S(1)}, bf16[256,192]{0,1:T(8,128)(2,1)}, u32[]{:S(2)}) copy-start(bf16[256,192]{0,1:T(8,128)(2,1)} %broadcast_select_fusion) | copy-start | bytes 294916
  456.4 163.2 %copy-start.7 = (bf16[256,192]{0,1:T(8,128)(2,1)S(1)}, bf16[256,192]{0,1:T(8,128)(2,1)}, u32[]{:S(2)}) copy-start(bf16[256,192]{0,1:T(8,128)(2,1)} %copy-done.6) | copy-start | bytes 294916
Sparse Core Ops, SparseCore 0:
  10.1 81.1 all-gather.5
  95.0 83.1 all-gather.3
  188.5 166.8 all-reduce.2
  360.3 82.6 all-gather.7
  452.7 166.8 all-reduce.4
  622.9 41.5 reduce-scatter.1
